TPU v7x, 32 devices: a whole 2x2x4 slice. The times are simulated.
32 devices in a mesh: prow: 8 (over z, x), pcol: 4 (over y, core).
Axes of the slice: x: 2, y: 2, z: 4, core: 2. Of those that a mesh axis runs over, the one named last changes fastest.
Arguments:
- inverse_pool: float32 [1536, 1536], P('prow', 'pcol'), may hold values from -6 to 6
- panel_one: float32 [1536, 512], P(('prow', 'pcol')), may hold values from -0.1875 to 0.1875
- panel_two: float32 [1536, 512], P(('prow', 'pcol')), may hold values from -0.21875 to 0.21875
- upper_two: float32 [512, 512], replicated, may hold values from -0.25 to 0.25
- lower_one: float32 [512, 512], replicated, as said below
- lower_two: float32 [512, 512], replicated, as said below
- list_one: int32 [9], replicated, may hold values from 0 to 11, as said below
- list_two: int32 [6], replicated, may hold values from 0 to 11, as said below
Outputs:
- first_offdiag: float32 [1536, 512], P(('prow', 'pcol'))
- first_diag: float32 [512, 512], replicated
- second_offdiag: float32 [1536, 512], P(('prow', 'pcol'))
- second_coupling: float32 [512, 512], replicated
- second_diag: float32 [512, 512], replicated
Inputs may be any that keep to these rules, and one draw needn't show every extreme that they name: `list_one`: distinct block numbers, among them 0, 6 and 11. `list_two`: distinct block numbers, each of which is also in list_one, among them 0, 6 and 11. `lower_one`: lower triangular with a diagonal of 1 to 1.5. `lower_two`: lower triangular with a diagonal of 1 to 1.5.
All inputs are finite; a program needn't handle non-finite values.
Results may differ from a plain program's by a relative error of at most 0.000073.
Values sent between devices are 32-bit elements; how exact they have to be, the bound alone decides.
A program may use at most 64 MiB of HBM per device.

v0:
```python
import jax
import jax.numpy as jnp
from jax import lax
from jax.sharding import PartitionSpec as P

BLK = 128


def product(left, right):
    return jnp.dot(left, right, precision=lax.Precision.HIGHEST, preferred_element_type=jnp.float32)


def transposed_product(left, right):
    return lax.dot_general(
        left,
        right,
        (((0,), (0,)), ((), ())),
        precision=lax.Precision.HIGHEST,
        preferred_element_type=jnp.float32,
    )


def live_rows(listing, first_row, count):
    row_ids = first_row + lax.iota(jnp.int32, count)
    blocks = row_ids // BLK
    hits = jnp.any(blocks[:, None] == listing[None, :], axis=1)
    return jnp.where(hits, 1.0, 0.0).astype(jnp.float32)[:, None]


def multiply_ancestors(inverse_tile, masked_span):
    groups = lax.axis_size("prow") // lax.axis_size("pcol")
    columns = lax.axis_size("pcol")
    span_rows = masked_span.shape[0]
    stacked = lax.all_gather(masked_span, "prow", axis=0, tiled=True)
    grouped = stacked.reshape(columns, groups * span_rows, masked_span.shape[1])
    regrouped = lax.all_to_all(grouped, "pcol", split_axis=0, concat_axis=0, tiled=True)
    accumulated = jnp.einsum(
        "rjkm,kjmw->rw",
        inverse_tile.reshape(inverse_tile.shape[0], groups, columns, span_rows),
        regrouped.reshape(columns, groups, span_rows, masked_span.shape[1]),
        precision=lax.Precision.HIGHEST,
        preferred_element_type=jnp.float32,
    )
    return lax.psum_scatter(accumulated, "pcol", scatter_dimension=0, tiled=True)


def local(inverse_pool, panel_one, panel_two, upper_two, lower_one, lower_two, list_one, list_two):
    span_rows = panel_one.shape[0]
    span_index = lax.axis_index("prow") * lax.axis_size("pcol") + lax.axis_index("pcol")
    first_row = span_index * span_rows
    live_one = live_rows(list_one, first_row, span_rows)
    live_two = live_rows(list_two, first_row, span_rows)
    masked_one = live_one * panel_one
    masked_two = live_two * panel_two
    first_offdiag = -live_one * multiply_ancestors(inverse_pool, masked_one)
    first_terms, coupling_terms = lax.psum(
        (
            transposed_product(masked_one, first_offdiag),
            transposed_product(first_offdiag, masked_two),
        ),
        ("prow", "pcol"),
    )
    second_product = multiply_ancestors(inverse_pool, masked_two)
    second_offdiag = -live_two * (product(first_offdiag, upper_two) + second_product)
    last_terms = lax.psum(transposed_product(masked_two, second_offdiag), ("prow", "pcol"))
    first_diag = transposed_product(lower_one, lower_one) - first_terms
    second_coupling = -(product(first_diag, upper_two) + coupling_terms)
    second_diag = (
        transposed_product(lower_two, lower_two)
        - transposed_product(upper_two, second_coupling)
        - last_terms
    )
    return (first_offdiag, first_diag, second_offdiag, second_coupling, second_diag)


def solution(mesh):
    return jax.shard_map(
        local,
        mesh=mesh,
        in_specs=(
            P("prow", "pcol"),
            P(("prow", "pcol"), None),
            P(("prow", "pcol"), None),
            P(),
            P(),
            P(),
            P(),
            P(),
        ),
        out_specs=(P(("prow", "pcol"), None), P(), P(("prow", "pcol"), None), P(), P()),
        check_vma=False,
    )
```

profile of v0, /device:TPU:0, one launch (start us, length us, event | category | flops | bytes accessed | tf_op | source)
XLA Modules:
  0.0 291.4 jit_solution(14642631012527775425)
XLA Ops:
  7.2 0.7 copy-done.10
  7.9 0.1 compare_reduce_fusion
  8.0 1.0 broadcast_multiply_fusion.1
  9.0 35.9 %all_gather.6 = f32[384,512]{1,0:T(8,128)} all-gather(f32[48,512]{1,0:T(8,128)S(1)} %broadcast_multiply_fusion.1), channel_id=1, replica_groups=mesh['prow'=8,'pcol'=4] {'prow'}, dimensions={0}, use_global_device_ids=true | all-gather | bytes 884736 | tf_op jit(solution)/shard_map/all_gather | solution.py:34
  44.9 3.6 %all-to-all-start = ((f32[4,96,512]{2,1,0:T(8,128)}), f32[4,96,512]{2,1,0:T(8,128)S(1)}, u32[]{:S(2)}, u32[]{:S(2)}) async-start(f32[4,96,512]{2,1,0:T(8,128)} %bitcast), calls=%async_computation | async-start | bytes 1572864 | tf_op jit(solution)/shard_map/all_to_all | solution.py:36
  48.6 0.0 reduce-scatter.3.cloned.1.call-start
  48.6 0.2 copy.20
  48.8 0.4 copy-done.11
  49.2 0.1 compare_reduce_fusion.1
  49.3 0.2 copy-done.9
  49.5 0.1 broadcast_multiply_fusion
  49.5 10.6 %all-to-all-done = f32[4,96,512]{2,1,0:T(8,128)S(1)} async-done(((f32[4,96,512]{2,1,0:T(8,128)}), f32[4,96,512]{2,1,0:T(8,128)S(1)}, u32[]{:S(2)}, u32[]{:S(2)}) %all-to-all-start) | async-done | bytes 786464 | tf_op jit(solution)/shard_map/all_to_all | solution.py:36
  60.1 1.6 convolution_bitcast_fusion.2
  61.8 0.0 reduce-scatter.5.cloned.1.call-start
  61.8 32.3 %all_gather.7 = f32[384,512]{1,0:T(8,128)S(1)} all-gather(f32[48,512]{1,0:T(8,128)S(1)} %broadcast_multiply_fusion), channel_id=1, replica_groups=mesh['prow'=8,'pcol'=4] {'prow'}, dimensions={0}, use_global_device_ids=true | all-gather | bytes 884736 | tf_op jit(solution)/shard_map/all_gather | solution.py:34
  94.1 14.0 %all_to_all.10 = f32[4,96,512]{2,1,0:T(8,128)S(1)} all-to-all(f32[4,96,512]{2,1,0:T(8,128)S(1)} %bitcast.45), channel_id=1, replica_groups=mesh['prow'=8,'pcol'=4] {'pcol'}, dimensions={0} | all-to-all | bytes 1572864 | tf_op jit(solution)/shard_map/all_to_all | solution.py:36
  108.2 1.6 convolution_bitcast_fusion.1
  109.8 0.2 all-reduce.3.cloned.1.call-start
  110.0 0.0 reduce-scatter.3.cloned.1.call-done
  110.1 1.0 broadcast_multiply_fusion.2
  111.0 2.0 fusion.8
  113.0 2.0 fusion.9
  115.0 15.5 %reduce-scatter.5.cloned.1.call-done = f32[48,512]{1,0:T(8,128)} async-done(((f32[192,512]{1,0:T(8,128)}), f32[48,512]{1,0:T(8,128)}) %reduce-scatter.5.cloned.1.call-update) | async-done | bytes 98320 | tf_op jit(solution)/shard_map/reduce_scatter | solution.py:44
  130.6 1.6 fusion.3
  132.2 2.0 fusion.11
  134.2 0.0 all-reduce.3.cloned.1.call-update
  134.3 1.2 copy-done.1
  135.5 1.9 fusion.10
  137.3 138.8 %all-reduce.3.cloned.1.call-done = (f32[512,512]{1,0:T(8,128)}, f32[512,512]{1,0:T(8,128)}, f32[512,512]{1,0:T(8,128)}) async-done(((f32[512,512]{1,0:T(8,128)}, f32[512,512]{1,0:T(8,128)}, f32[512,512]{1,0:T(8,128)}), (f32[512,512]{1,0:T(8,128)}, f32[512,512]{1,0:T(8,128)}, f32[512,512]{1,0:T(8,128)})) %all-reduce.3.cloned.1.call-update) | async-done | bytes 3145744 | tf_op jit(solution)/shard_map/psum | solution.py:56
  276.2 3.8 %convolution_subtract_fusion = f32[512,512]{1,0:T(8,128)S(1)} fusion(f32[512,512]{1,0:T(8,128)} %get-tuple-element.5, f32[512,512]{1,0:T(8,128)} %param.12), kind=kOutput, calls=%fused_computation.5 | convolution fusion | flops 1610874880 | bytes 3145728 | tf_op jit(solution)/shard_map/dot_general | solution.py:14
  280.0 1.9 fusion.2
  282.0 2.9 fusion.1
  (25 shorter events, 0.1 us)
Async XLA Ops:
  7.2 123.4 %copy-start = (f32[512,512]{1,0:T(8,128)S(1)}, f32[512,512]{1,0:T(8,128)}, u32[]{:S(2)}) copy-start(f32[512,512]{1,0:T(8,128)} %param.11) | copy-start | bytes 3145732
  7.2 0.7 copy-start.10
  44.9 3.7 %copy-start.8 = (f32[192,384]{1,0:T(8,128)S(1)}, f32[192,384]{1,0:T(8,128)}, u32[]{:S(2)}) copy-start(f32[192,384]{1,0:T(8,128)} %param.8) | copy-start | bytes 884740
  44.9 15.2 %all-to-all-start = ((f32[4,96,512]{2,1,0:T(8,128)}), f32[4,96,512]{2,1,0:T(8,128)S(1)}, u32[]{:S(2)}, u32[]{:S(2)}) async-start(f32[4,96,512]{2,1,0:T(8,128)} %bitcast), calls=%async_computation | async-start | bytes 1572864 | tf_op jit(solution)/shard_map/all_to_all | solution.py:36
  48.5 0.7 copy-start.11
  48.6 0.9 copy-start.9
  48.6 61.5 %reduce-scatter.3.cloned.1.call-start = ((), (), s32[]{:S(2)}) async-start(), calls=%async_computation.4 | async-start | bytes 491520 | tf_op jit(solution)/shard_map/reduce_scatter | solution.py:44
  61.8 68.8 %reduce-scatter.5.cloned.1.call-start = ((), (), s32[]{:S(2)}) async-start(), calls=%async_computation.5 | async-start | bytes 491520 | tf_op jit(solution)/shard_map/reduce_scatter | solution.py:44
  109.8 166.4 %all-reduce.3.cloned.1.call-start = ((), (), s32[]{:S(2)}) async-start(), calls=%async_computation.6 | async-start | bytes 6291456 | tf_op jit(solution)/shard_map/psum | solution.py:56
  111.0 19.6 %copy-start.4 = (f32[48,512]{1,0:T(8,128)}, f32[48,512]{1,0:T(8,128)S(1)}, u32[]{:S(2)}) copy-start(f32[48,512]{1,0:T(8,128)S(1)} %broadcast_multiply_fusion.2) | copy-start | bytes 294916
  132.2 2.0 copy-start.7
  134.2 1.2 copy-start.1
  276.2 3.8 %copy-start.6 = (f32[512,512]{1,0:T(8,128)S(1)}, f32[512,512]{1,0:T(8,128)}, u32[]{:S(2)}) copy-start(f32[512,512]{1,0:T(8,128)} %get-tuple-element.6) | copy-start | bytes 3145732
  280.0 2.0 copy-start.3
  280.0 2.0 copy-start.5
  282.0 2.9 copy-start.2
Sparse Core Ops, SparseCore 0:
  61.9 20.7 reduce-scatter.2
  109.9 20.6 reduce-scatter.4
  137.0 139.1 all-reduce.2
where the time goes:
time: 292 us; the launch traced here: 291 us
  waiting for transfers between devices  165 us (57%)
  blocking collectives  82.2 us (28%)
  matrix products  21.3 us (7%)
  between operations  13.9 us (5%)
  starting transfers between devices  3.93 us (1%)
    psum x1, waiting for transfers between devices, local(): lax.psum((transposed_product(masked_one, first_offdiag), transposed_produ...  139 us
    all_gather x2, blocking collectives, multiply_ancestors(): stacked = lax.all_gather(masked_span, 'prow', axis=0, tiled=True)  68.2 us
    reduce_scatter x2, waiting for transfers between devices, multiply_ancestors(): lax.psum_scatter(accumulated, 'pcol', scatter_dimension=0, tiled=True)  15.6 us
    dot_general x6, matrix products, transposed_product(): lax.dot_general(left, right, (((0,), (0,)), ((), ())), precision=lax.Prec...  14.5 us
    all_to_all x1, blocking collectives, multiply_ancestors(): lax.all_to_all(grouped, 'pcol', split_axis=0, concat_axis=0, tiled=True)  14 us
    all_to_all x1, waiting for transfers between devices, multiply_ancestors(): lax.all_to_all(grouped, 'pcol', split_axis=0, concat_axis=0, tiled=True)  10.6 us
  transfers between devices with their start and end apart: 4, of which 3 were waited for; matrix products, arithmetic and copies ran while one was open for 3% of the time, Pallas kernels for 0%

commit v1 on v0

v1 whole, which is shorter than its diff:
```python
import functools

import jax
import jax.numpy as jnp
from jax import lax
from jax.experimental import pallas as pl
from jax.experimental.pallas import tpu as pltpu
from jax.sharding import PartitionSpec as P

BLK = 128
MESH = pl.DeviceIdType.MESH


def halves(value):
    high = value.astype(jnp.bfloat16)
    low = (value - high.astype(jnp.float32)).astype(jnp.bfloat16)
    return high, low


def split_dot(left, right, dims):
    def one(a, b):
        return lax.dot_general(a, b, (dims, ((), ())), preferred_element_type=jnp.float32)

    return one(left[0], right[0]) + (one(left[0], right[1]) + one(left[1], right[0]))


PLAIN = ((1,), (0,))
FIRST = ((0,), (0,))


def live_column(listing, first_row, count):
    blocks = (first_row + lax.broadcasted_iota(jnp.int32, (count, 1), 0)) // BLK

    def step(k, hits):
        return jnp.maximum(hits, jnp.where(blocks == listing[k], 1.0, 0.0).astype(jnp.float32))

    return lax.fori_loop(0, listing.shape[0], step, jnp.zeros((count, 1), jnp.float32))


def body(
    R, C, nsend,
    x_in, one_in, two_in, u_in, l1_in, l2_in, list1, list2,
    f_out, d1_out, s_out, c_out, d2_out,
    x_v, u_v, l1_v, l2_v, zbuf, mcol, mrow, abuf, arecv, asum, frow, qbuf, qrecv, qfull, wt,
    load_sem, send_sem, z_sem, m_sem, g_sem, a_sem, f_sem, q_sem, gz_sem, gx_sem, gy_sem, gc_sem,
):
    g = R // C
    span, W = one_in.shape
    rows, K = x_in.shape
    wc = W // C
    ch = 3 * W // R
    p, c = lax.axis_index("prow"), lax.axis_index("pcol")
    z, i = p // g, p % g
    partner = c + 1 - 2 * (c % 2)
    panels = (one_in, two_in)
    pending = []

    def remote(src, dst, recv_sem, to):
        return pltpu.make_async_remote_copy(
            src_ref=src, dst_ref=dst, send_sem=send_sem.at[len(pending)],
            recv_sem=recv_sem, device_id=to, device_id_type=MESH,
        )

    def send(src, dst, recv_sem, to, when=None):
        copy = remote(src, dst, recv_sem, to)
        pending.append((copy, when))
        if when is None:
            copy.start()
        else:
            pl.when(when)(copy.start)

    def arrived(dst, recv_sem):
        pltpu.make_async_copy(dst, dst, recv_sem).wait()

    def at(base, index, size):
        return base.at[pl.ds(pl.multiple_of(index * size, 8), size)]

    loads = []
    for k, (src, dst) in enumerate(((x_in, x_v), (l1_in, l1_v), (l2_in, l2_v), (u_in, u_v))):
        copy = pltpu.make_async_copy(src, dst, load_sem.at[k])
        copy.start()
        loads.append(copy)

    barrier = pltpu.get_barrier_semaphore()
    peers = 0
    for dp in range(1, R):
        pl.semaphore_signal(barrier, inc=1, device_id=((p + dp) % R, c), device_id_type=MESH)
        peers += 1
    for di in range(g):
        for dc in range(1, C):
            pl.semaphore_signal(
                barrier, inc=1, device_id=(z * g + (i + di) % g, (c + dc) % C), device_id_type=MESH
            )
            peers += 1
    pl.semaphore_wait(barrier, peers)

    for k in range(2):
        for dz in range(1, C):
            send(panels[k], zbuf.at[k, dz], z_sem.at[k, dz], (((z + dz) % C) * g + i, c))

    own = i * C + c

    def to_columns(k, dz):
        plane = (z + C - dz) % C
        src = panels[k] if dz == 0 else zbuf.at[k, dz]
        dst, sem = at(mcol.at[k], own, span), m_sem.at[k, own]
        for di in range(g):
            to = (z * g + (i + di) % g, plane)
            if di:
                send(src, dst, sem, to)
            else:
                send(src, dst, sem, to, plane != c)
                pl.when(plane == c)(pltpu.make_async_copy(src, dst, sem).start)

    for k in range(2):
        to_columns(k, 0)
    for k in range(2):
        for dz in range(1, C):
            arrived(zbuf.at[k, dz], z_sem.at[k, dz])
            to_columns(k, dz)

    for k in range(2):
        dst, sem = at(mrow.at[k], c, span), g_sem.at[k, c]
        pltpu.make_async_copy(panels[k], dst, sem).start()
        for dc in range(2, C, 2):
            send(panels[k], dst, sem, (p, (c + dc) % C))
        send(panels[k], dst, sem, (p, partner))

    for copy in loads:
        copy.wait()
    for src, dst in ((l1_v, d1_out), (l2_v, d2_out)):
        pair = halves(src[...])
        dst[...] = split_dot(pair, pair, FIRST)

    for k in range(2):
        for dc in range(2, C, 2):
            other = (c + dc) % C
            piece = at(mrow.at[k], other, span)
            arrived(piece, g_sem.at[k, other])
            send(piece, piece, g_sem.at[k, other], (p, partner))

    x_pair = halves(x_v[...])
    for k, listing in enumerate((list1, list2)):
        for j in range(g * C):
            arrived(mcol.at[k, pl.ds(j * span, span)], m_sem.at[k, j])
        masked = live_column(listing, c * K, K) * mcol[k]
        product = split_dot(x_pair, halves(masked), PLAIN)
        for cc in range(C):
            abuf[k, cc] = product[:, cc * wc:(cc + 1) * wc]
        for dc in range(1, C):
            other = (c + dc) % C
            send(abuf.at[k, other], arecv.at[k, dc], a_sem.at[k, dc], (p, other))

    row_one, row_two = live_column(list1, p * rows, rows), live_column(list2, p * rows, rows)
    for k in range(2):
        arrived(at(mrow.at[k], c, span), g_sem.at[k, c])
        for dc in range(0, C, 2):
            other = (partner + dc) % C
            arrived(at(mrow.at[k], other, span), g_sem.at[k, other])
    left_one = halves(row_one * mrow[0])
    left_two = halves(row_two * mrow[1])

    def total(k, mask):
        result = abuf[k, c]
        for dc in range(1, C):
            arrived(arecv.at[k, dc], a_sem.at[k, dc])
            result = result + arecv[k, dc]
        result = mask * result
        asum[k] = result
        return halves(result)

    right = total(0, row_one)
    qbuf[0:W] = split_dot(left_one, right, FIRST)
    cross = split_dot(right, left_two, FIRST)
    for cc in range(C):
        qbuf[W + cc * wc:W + (cc + 1) * wc] = cross[:, cc * wc:(cc + 1) * wc]
    right = total(1, row_two)
    qbuf[2 * W:3 * W] = split_dot(left_two, right, FIRST)

    for dp in range(1, R):
        other = (p + dp) % R
        send(at(qbuf, other, ch), qrecv.at[dp], q_sem.at[dp], (other, c))
    for k in range(2):
        for dc in range(1, C):
            other = (c + dc) % C
            send(at(asum.at[k], other, span), frow.at[k, c], f_sem.at[k, c], (p, other))
        frow[k, c] = asum[k, pl.ds(pl.multiple_of(c * span, 8), span)]

    result = qbuf[pl.ds(pl.multiple_of(p * ch, 8), ch)]
    for dp in range(1, R):
        arrived(qrecv.at[dp], q_sem.at[dp])
        result = result + qrecv[dp]
    qfull[c, pl.ds(pl.multiple_of(p * ch, 8), ch)] = result

    def chunk(dz, di, dc, base):
        rank = ((z + C - dz) % C) * g + (i + g - di) % g
        return at(qfull.at[(base + C - dc) % C], rank, ch)

    def onward(dz, di):
        piece = chunk(dz, di, 0, c)
        for dc in range(2, C, 2):
            send(piece, piece, gy_sem.at[dz, di, dc // 2], (p, (c + dc) % C))
        send(piece, piece, gc_sem.at[dz, di, 0], (p, partner))

    piece = chunk(0, 0, 0, c)
    for dz in range(1, C):
        send(piece, piece, gz_sem.at[dz], (((z + dz) % C) * g + i, c))
    for dz in range(C):
        piece = chunk(dz, 0, 0, c)
        if dz:
            arrived(piece, gz_sem.at[dz])
        for di in range(1, g):
            send(piece, piece, gx_sem.at[dz, di], (z * g + (i + di) % g, c))
        onward(dz, 0)
    for dz in range(C):
        for di in range(1, g):
            arrived(chunk(dz, di, 0, c), gx_sem.at[dz, di])
            onward(dz, di)

    u_pair = halves(u_v[...])
    for k in range(2):
        for dc in range(1, C):
            other = (c + dc) % C
            arrived(frow.at[k, other], f_sem.at[k, other])
    first_row = p * rows + c * span
    for cc in range(C):
        f_out[:, cc * wc:(cc + 1) * wc] = -frow[0, cc]
        s_out[:, cc * wc:(cc + 1) * wc] = frow[1, cc]
    f_u = split_dot(halves(f_out[...]), u_pair, PLAIN)
    s_out[...] = -live_column(list2, first_row, span) * (f_u + s_out[...])

    for dz in range(C):
        for di in range(g):
            for dc in range(2, C, 2):
                piece = chunk(dz, di, dc, c)
                arrived(piece, gy_sem.at[dz, di, dc // 2])
                send(piece, piece, gc_sem.at[dz, di, dc // 2], (p, partner))
    for dz in range(C):
        for di in range(g):
            for dc in range(0, C, 2):
                arrived(chunk(dz, di, dc, partner), gc_sem.at[dz, di, dc // 2])

    for cc in range(C):
        lanes = slice(cc * wc, (cc + 1) * wc)
        d1_out[:, lanes] += qfull[cc, 0:W]
        for k in range(C):
            wt[lanes, k * wc:(k + 1) * wc] = qfull[cc, W + k * wc:W + (k + 1) * wc]
        d2_out[:, lanes] += qfull[cc, 2 * W:3 * W]
    c_out[...] = wt[...] - split_dot(halves(d1_out[...]), u_pair, PLAIN)
    d2_out[...] -= split_dot(u_pair, halves(c_out[...]), FIRST) + split_dot(
        halves(wt[...]), u_pair, FIRST
    )

    assert len(pending) == nsend
    for copy, when in pending:
        if when is None:
            copy.wait_send()
        else:
            pl.when(when)(copy.wait_send)


def solution(mesh):
    R, C = mesh.shape["prow"], mesh.shape["pcol"]
    g = R // C

    def local(inverse_pool, panel_one, panel_two, upper_two, lower_one, lower_two, list_one, list_two):
        span, W = panel_one.shape
        rows, K = inverse_pool.shape
        wc, ch = W // C, 3 * W // R
        half = C // 2
        nsend = (
            2 * (C - 1) + 2 * C * g + 2 * half + 2 * (half - 1) + 2 * (C - 1) + (R - 1) + 2 * (C - 1)
            + (C - 1) + C * (g - 1) + C * g * half + C * g * (half - 1)
        )
        f32, dma = jnp.float32, pltpu.SemaphoreType.DMA
        block = jax.ShapeDtypeStruct((W, W), f32)
        strip = jax.ShapeDtypeStruct((span, W), f32)
        return pl.pallas_call(
            functools.partial(body, R, C, nsend),
            out_shape=(strip, block, strip, block, block),
            in_specs=[pl.BlockSpec(memory_space=pl.ANY)] * 6
            + [pl.BlockSpec(memory_space=pltpu.SMEM)] * 2,
            out_specs=(pl.BlockSpec(memory_space=pltpu.VMEM),) * 5,
            scratch_shapes=[
                pltpu.VMEM((rows, K), f32),
                pltpu.VMEM((W, W), f32),
                pltpu.VMEM((W, W), f32),
                pltpu.VMEM((W, W), f32),
                pltpu.VMEM((2, C, span, W), f32),
                pltpu.VMEM((2, K, W), f32),
                pltpu.VMEM((2, rows, W), f32),
                pltpu.VMEM((2, C, rows, wc), f32),
                pltpu.VMEM((2, C, rows, wc), f32),
                pltpu.VMEM((2, rows, wc), f32),
                pltpu.VMEM((2, C, span, wc), f32),
                pltpu.VMEM((3 * W, wc), f32),
                pltpu.VMEM((R, ch, wc), f32),
                pltpu.VMEM((C, 3 * W, wc), f32),
                pltpu.VMEM((W, W), f32),
                dma((4,)),
                dma((nsend,)),
                dma((2, C)),
                dma((2, g * C)),
                dma((2, C)),
                dma((2, C)),
                dma((2, C)),
                dma((R,)),
                dma((C,)),
                dma((C, g)),
                dma((C, g, half)),
                dma((C, g, half)),
            ],
            compiler_params=pltpu.CompilerParams(collective_id=0, has_side_effects=True),
        )(inverse_pool, panel_one, panel_two, upper_two, lower_one, lower_two, list_one, list_two)

    return jax.shard_map(
        local,
        mesh=mesh,
        in_specs=(
            P("prow", "pcol"),
            P(("prow", "pcol"), None),
            P(("prow", "pcol"), None),
            P(),
            P(),
            P(),
            P(),
            P(),
        ),
        out_specs=(P(("prow", "pcol"), None), P(), P(("prow", "pcol"), None), P(), P()),
        check_vma=False,
    )
```

time: 292 us -> 108 us (0.37)
  the two profiles are of different devices: /device:TPU:0 before, /device:TPU:7 now
where the time goes in v1:
time: 108 us
  Pallas kernels  99.8 us (92%)
  local copies, waits for them, and re-layouts  7.12 us (7%)
    pallas_call x1, Pallas kernels, local(): pl.pallas_call(functools.partial(body, R, C, nsend), out_shape=(strip, bl...  99.8 us
    unnamed x11, local copies, waits for them, and re-layouts  7.12 us

profile of v1, /device:TPU:7, one launch (start us, length us, event | category | flops | bytes accessed | tf_op | source)
XLA Modules:
  0.0 107.6 jit_solution(4791590857549972685)
XLA Ops:
  0.6 99.8 %shard_map.119 = (f32[48,512]{1,0:T(8,128)}, f32[512,512]{1,0:T(8,128)}, f32[48,512]{1,0:T(8,128)}, f32[512,512]{1,0:T(8,128)}, f32[512,512]{1,0:T(8,128)}) custom-call(f32[192,384]{1,0:T(8,128)} %x_in.1, f32[48,512]{1,0:T(8,128)} %one_in.1, f32[48,512]{1,0:T(8,128)} %two_in.1, f32[512,512]{1,0:T(8,128)} %u_in.1, f32[512,512]{1,0:T(8,128)} %l1_in.1, ...), custom_call_target="tpu_custom_call" | custom-call | tf_op jit(solution)/shard_map/pallas_call | solution.py:278
  100.4 1.5 %copy.18 = f32[48,512]{1,0:T(8,128)} copy(f32[48,512]{1,0:T(8,128)} %get-tuple-element.10) | data formatting | bytes 196608
  102.0 0.0 copy-start.2
  102.0 0.0 copy-start.1
  102.0 2.4 %copy.19 = f32[512,512]{1,0:T(8,128)} copy(f32[512,512]{1,0:T(8,128)} %get-tuple-element.11) | data formatting | bytes 2097152
  104.3 0.0 copy-done.2
  104.3 0.6 copy.20
  105.0 0.0 copy-done.1
  105.0 0.0 copy-start
  105.0 1.0 copy.21
  106.0 0.6 copy-done
  106.6 1.0 copy.22
Async XLA Ops:
  102.0 2.4 %copy-start.2 = (f32[48,512]{1,0:T(8,128)S(1)}, f32[48,512]{1,0:T(8,128)}, u32[]{:S(2)}) copy-start(f32[48,512]{1,0:T(8,128)} %get-tuple-element.12) | copy-start | bytes 294916
  102.0 3.0 %copy-start.1 = (f32[512,512]{1,0:T(8,128)S(1)}, f32[512,512]{1,0:T(8,128)}, u32[]{:S(2)}) copy-start(f32[512,512]{1,0:T(8,128)} %get-tuple-element.13) | copy-start | bytes 3145732
  105.0 1.6 %copy-start = (f32[512,512]{1,0:T(8,128)S(1)}, f32[512,512]{1,0:T(8,128)}, u32[]{:S(2)}) copy-start(f32[512,512]{1,0:T(8,128)} %get-tuple-element.14) | copy-start | bytes 3145732

commit v2 on v1

v2 whole, which is shorter than its diff:
```python
import functools

import jax
import jax.numpy as jnp
from jax import lax
from jax.experimental import pallas as pl
from jax.experimental.pallas import tpu as pltpu
from jax.sharding import PartitionSpec as P

BLK = 128
MESH = pl.DeviceIdType.MESH


def halves(value):
    high = value.astype(jnp.bfloat16)
    low = (value - high.astype(jnp.float32)).astype(jnp.bfloat16)
    return high, low


def split_dot(left, right, dims):
    def one(a, b):
        return lax.dot_general(a, b, (dims, ((), ())), preferred_element_type=jnp.float32)

    return one(left[0], right[0]) + (one(left[0], right[1]) + one(left[1], right[0]))


PLAIN = ((1,), (0,))
FIRST = ((0,), (0,))


def live_column(listing, first_row, count):
    blocks = (first_row + lax.broadcasted_iota(jnp.int32, (count, 1), 0)) // BLK

    def step(k, hits):
        return jnp.maximum(hits, jnp.where(blocks == listing[k], 1.0, 0.0).astype(jnp.float32))

    return lax.fori_loop(0, listing.shape[0], step, jnp.zeros((count, 1), jnp.float32))


def body(
    R, C, nsend,
    x_in, one_in, two_in, u_in, l1_in, l2_in, list1, list2,
    f_out, d1_out, s_out, c_out, d2_out,
    x_v, u_v, l1_v, l2_v, zbuf, mcol, mrow, abuf, arecv, brecv, asum, frow, qbuf, xrecv, xsum, zrecv, qfull, wt,
    load_sem, send_sem, z_sem, m_sem, g_sem, a_sem, b_sem, f_sem, x_sem, q_sem, gz_sem, gx_sem, gy_sem, gc_sem,
):
    g, half = R // C, C // 2
    span, W = one_in.shape
    rows, K = x_in.shape
    wc = W // C
    part, ch = W // g, W // R
    p, c = lax.axis_index("prow"), lax.axis_index("pcol")
    z, i = p // g, p % g
    partner = c + 1 - 2 * (c % 2)
    panels = (one_in, two_in)
    pending = []

    def send(src, dst, recv_sem, to, when=None):
        copy = pltpu.make_async_remote_copy(
            src_ref=src, dst_ref=dst, send_sem=send_sem.at[len(pending)],
            recv_sem=recv_sem, device_id=to, device_id_type=MESH,
        )
        pending.append((copy, when))
        if when is None:
            copy.start()
        else:
            pl.when(when)(copy.start)

    def arrived(dst, recv_sem):
        pltpu.make_async_copy(dst, dst, recv_sem).wait()

    def at(base, index, size):
        return base.at[pl.ds(pl.multiple_of(index * size, 8), size)]

    def plane_peer(dz):
        return (((z + dz) % C) * g + i, c)

    def side_peer(di):
        return (z * g + (i + di) % g, c)

    loads = []
    for k, (src, dst) in enumerate(((l1_in, l1_v), (l2_in, l2_v), (x_in, x_v), (u_in, u_v))):
        copy = pltpu.make_async_copy(src, dst, load_sem.at[k])
        copy.start()
        loads.append(copy)

    barrier = pltpu.get_barrier_semaphore()
    peers = 0
    for dp in range(1, R):
        pl.semaphore_signal(barrier, inc=1, device_id=((p + dp) % R, c), device_id_type=MESH)
        peers += 1
    for di in range(g):
        for dc in range(1, C):
            pl.semaphore_signal(
                barrier, inc=1, device_id=(z * g + (i + di) % g, (c + dc) % C), device_id_type=MESH
            )
            peers += 1
    pl.semaphore_wait(barrier, peers)

    def to_columns(k, dz):
        plane = (z + C - dz) % C
        src = panels[k] if dz == 0 else zbuf.at[k, dz]
        own = i * C + c
        dst, sem = at(mcol.at[k], own, span), m_sem.at[k, own]
        send(src, dst, sem, (p, plane), plane != c)
        pl.when(plane == c)(pltpu.make_async_copy(src, dst, sem).start)
        for di in range(1, g):
            send(src, dst, sem, (z * g + (i + di) % g, plane), plane // 2 == c // 2)

    def far(dy, parity):
        return ((c // 2 + dy) % half) * 2 + parity

    def across(k):
        for dy in range(1, half):
            for parity in range(2):
                slot = i * C + far(dy, parity)
                piece = at(mcol.at[k], slot, span)
                arrived(piece, m_sem.at[k, slot])
                for di in range(1, g):
                    send(piece, piece, m_sem.at[k, slot], side_peer(di))

    def columns_arrived(k):
        for dy in range(half):
            for parity in range(2):
                for di in range(1 if dy else 0, g):
                    slot = ((i + di) % g) * C + far(dy, parity)
                    arrived(at(mcol.at[k], slot, span), m_sem.at[k, slot])

    def to_row(k):
        dst, sem = at(mrow.at[k], c, span), g_sem.at[k, c]
        pltpu.make_async_copy(panels[k], dst, sem).start()
        for dc in range(2, C, 2):
            send(panels[k], dst, sem, (p, (c + dc) % C))
        send(panels[k], dst, sem, (p, partner))

    def row_onward(k):
        for dc in range(2, C, 2):
            other = (c + dc) % C
            piece = at(mrow.at[k], other, span)
            arrived(piece, g_sem.at[k, other])
            send(piece, piece, g_sem.at[k, other], (p, partner))

    def row_arrived(k):
        arrived(at(mrow.at[k], c, span), g_sem.at[k, c])
        for dc in range(0, C, 2):
            other = (partner + dc) % C
            arrived(at(mrow.at[k], other, span), g_sem.at[k, other])

    def tile_product(k, listing):
        columns_arrived(k)
        masked = live_column(listing, c * K, K) * mcol[k]
        product = split_dot(x_pair, halves(masked), PLAIN)
        for cc in range(C):
            abuf[k, cc] = product[:, cc * wc:(cc + 1) * wc]
        for j in range(half):
            send(abuf.at[k, (partner + 2 * j) % C], arecv.at[k, j], a_sem.at[k, j], (p, partner))

    def pair_sum(k):
        for j in list(range(1, half)) + [0]:
            other = (c + 2 * j) % C
            arrived(arecv.at[k, j], a_sem.at[k, j])
            abuf[k, other] = abuf[k, other] + arecv[k, j]
            if j:
                send(abuf.at[k, other], brecv.at[k, j], b_sem.at[k, j], (p, other))

    def total(k, mask):
        result = abuf[k, c]
        for j in range(1, half):
            arrived(brecv.at[k, j], b_sem.at[k, j])
            result = result + brecv[k, j]
        result = mask * result
        asum[k] = result
        return halves(result)

    def rows_out(k):
        for dc in range(1, C):
            other = (c + dc) % C
            send(at(asum.at[k], other, span), frow.at[k, c], f_sem.at[k, c], (p, other))
        frow[k, c] = asum[k, pl.ds(pl.multiple_of(c * span, 8), span)]

    def side_out(b):
        for di in range(1, g):
            other = (i + di) % g
            send(at(qbuf.at[b], other, part), xrecv.at[b, di], x_sem.at[b, di], side_peer(di))

    def side_in(b):
        result = qbuf[b, pl.ds(pl.multiple_of(i * part, 8), part)]
        for di in range(1, g):
            arrived(xrecv.at[b, di], x_sem.at[b, di])
            result = result + xrecv[b, di]
        xsum[b] = result
        for dz in range(1, C):
            send(at(xsum.at[b], (z + dz) % C, ch), zrecv.at[b, dz], q_sem.at[b, dz], plane_peer(dz))

    def block(b, column, side, plane):
        first = b * W + side * part + plane * ch
        return qfull.at[column, pl.ds(pl.multiple_of(first, 8), ch)]

    def block_part(b, column, side):
        return qfull.at[column, pl.ds(pl.multiple_of(b * W + side * part, 8), part)]

    def plane_in(b):
        result = xsum[b, pl.ds(pl.multiple_of(z * ch, 8), ch)]
        for dz in range(1, C):
            arrived(zrecv.at[b, dz], q_sem.at[b, dz])
            result = result + zrecv[b, dz]
        piece = block(b, c, i, z)
        piece[...] = result
        for dz in range(1, C):
            send(piece, piece, gz_sem.at[b, dz], plane_peer(dz))

    def onward(b, di):
        piece = block_part(b, c, (i + g - di) % g)
        for dc in range(2, C, 2):
            send(piece, piece, gy_sem.at[b, di, dc // 2], (p, (c + dc) % C))
        send(piece, piece, gc_sem.at[b, di, 0], (p, partner))

    def gather_side(b):
        for dz in range(1, C):
            arrived(block(b, c, i, (z + C - dz) % C), gz_sem.at[b, dz])
        piece = block_part(b, c, i)
        for di in range(1, g):
            send(piece, piece, gx_sem.at[b, di], side_peer(di))
        onward(b, 0)

    def gather_row(b):
        for di in range(1, g):
            arrived(block_part(b, c, (i + g - di) % g), gx_sem.at[b, di])
            onward(b, di)

    def gather_core(b):
        for di in range(g):
            for dc in range(2, C, 2):
                piece = block_part(b, (c + C - dc) % C, (i + g - di) % g)
                arrived(piece, gy_sem.at[b, di, dc // 2])
                send(piece, piece, gc_sem.at[b, di, dc // 2], (p, partner))

    def gathered(b):
        for di in range(g):
            for dc in range(0, C, 2):
                piece = block_part(b, (partner + C - dc) % C, (i + g - di) % g)
                arrived(piece, gc_sem.at[b, di, dc // 2])

    for k in range(2):
        for dz in range(1, C):
            send(panels[k], zbuf.at[k, dz], z_sem.at[k, dz], plane_peer(dz))
        to_columns(k, 0)
    for copy in loads[:2]:
        copy.wait()
    for src, dst in ((l1_v, d1_out), (l2_v, d2_out)):
        pair = halves(src[...])
        dst[...] = split_dot(pair, pair, FIRST)
    for k in range(2):
        for dz in range(1, C):
            arrived(zbuf.at[k, dz], z_sem.at[k, dz])
            to_columns(k, dz)
        to_row(k)
        if k == 0:
            across(0)
            for copy in loads[2:]:
                copy.wait()
            x_pair = halves(x_v[...])
            row_one, row_two = live_column(list1, p * rows, rows), live_column(list2, p * rows, rows)
    row_onward(0)
    tile_product(0, list1)
    across(1)
    pair_sum(0)
    row_onward(1)
    row_arrived(0)
    left = halves(row_one * mrow[0])
    right_one = total(0, row_one)
    qbuf[0] = split_dot(left, right_one, FIRST)
    side_out(0)
    tile_product(1, list2)
    pair_sum(1)
    row_arrived(1)
    left = halves(row_two * mrow[1])
    cross = split_dot(right_one, left, FIRST)
    for cc in range(C):
        qbuf[1, cc * wc:(cc + 1) * wc] = cross[:, cc * wc:(cc + 1) * wc]
    side_out(1)
    side_in(0)
    right_two = total(1, row_two)
    qbuf[2] = split_dot(left, right_two, FIRST)
    side_out(2)
    plane_in(0)
    side_in(1)
    gather_side(0)
    plane_in(1)
    side_in(2)
    gather_row(0)
    gather_side(1)
    plane_in(2)
    gather_core(0)
    gather_row(1)
    gather_side(2)
    rows_out(0)
    rows_out(1)
    gather_core(1)
    gather_row(2)

    u_pair = halves(u_v[...])
    gathered(0)
    for cc in range(C):
        d1_out[:, cc * wc:(cc + 1) * wc] += qfull[cc, 0:W]
    d1_u = split_dot(halves(d1_out[...]), u_pair, PLAIN)
    gather_core(2)
    for k in range(2):
        for dc in range(1, C):
            other = (c + dc) % C
            arrived(frow.at[k, other], f_sem.at[k, other])
    for cc in range(C):
        f_out[:, cc * wc:(cc + 1) * wc] = -frow[0, cc]
        s_out[:, cc * wc:(cc + 1) * wc] = frow[1, cc]
    f_u = split_dot(halves(f_out[...]), u_pair, PLAIN)
    s_out[...] = -live_column(list2, p * rows + c * span, span) * (f_u + s_out[...])

    gathered(1)
    for cc in range(C):
        for k in range(C):
            wt[cc * wc:(cc + 1) * wc, k * wc:(k + 1) * wc] = qfull[cc, W + k * wc:W + (k + 1) * wc]
    c_out[...] = wt[...] - d1_u
    d2_out[...] -= split_dot(u_pair, halves(c_out[...]), FIRST) + split_dot(
        halves(wt[...]), u_pair, FIRST
    )
    gathered(2)
    for cc in range(C):
        d2_out[:, cc * wc:(cc + 1) * wc] += qfull[cc, 2 * W:3 * W]

    assert len(pending) == nsend, len(pending)
    for copy, when in pending:
        if when is None:
            copy.wait_send()
        else:
            pl.when(when)(copy.wait_send)


def solution(mesh):
    R, C = mesh.shape["prow"], mesh.shape["pcol"]
    g = R // C

    def local(inverse_pool, panel_one, panel_two, upper_two, lower_one, lower_two, list_one, list_two):
        span, W = panel_one.shape
        rows, K = inverse_pool.shape
        wc, half = W // C, C // 2
        panel = (C - 1) + C * g + 2 * (half - 1) * (g - 1) + half + (half - 1)
        reduced = half + (half - 1) + (C - 1)
        gram = (g - 1) + 2 * (C - 1) + (g - 1) + g * half + g * (half - 1)
        nsend = 2 * panel + 2 * reduced + 3 * gram
        f32, dma = jnp.float32, pltpu.SemaphoreType.DMA
        block = jax.ShapeDtypeStruct((W, W), f32)
        strip = jax.ShapeDtypeStruct((span, W), f32)
        return pl.pallas_call(
            functools.partial(body, R, C, nsend),
            out_shape=(strip, block, strip, block, block),
            in_specs=[pl.BlockSpec(memory_space=pl.ANY)] * 6
            + [pl.BlockSpec(memory_space=pltpu.SMEM)] * 2,
            out_specs=(pl.BlockSpec(memory_space=pltpu.VMEM),) * 5,
            scratch_shapes=[
                pltpu.VMEM((rows, K), f32),
                pltpu.VMEM((W, W), f32),
                pltpu.VMEM((W, W), f32),
                pltpu.VMEM((W, W), f32),
                pltpu.VMEM((2, C, span, W), f32),
                pltpu.VMEM((2, K, W), f32),
                pltpu.VMEM((2, rows, W), f32),
                pltpu.VMEM((2, C, rows, wc), f32),
                pltpu.VMEM((2, half, rows, wc), f32),
                pltpu.VMEM((2, half, rows, wc), f32),
                pltpu.VMEM((2, rows, wc), f32),
                pltpu.VMEM((2, C, span, wc), f32),
                pltpu.VMEM((3, W, wc), f32),
                pltpu.VMEM((3, g, W // g, wc), f32),
                pltpu.VMEM((3, W // g, wc), f32),
                pltpu.VMEM((3, C, W // R, wc), f32),
                pltpu.VMEM((C, 3 * W, wc), f32),
                pltpu.VMEM((W, W), f32),
                dma((4,)),
                dma((nsend,)),
                dma((2, C)),
                dma((2, g * C)),
                dma((2, C)),
                dma((2, half)),
                dma((2, half)),
                dma((2, C)),
                dma((3, g)),
                dma((3, C)),
                dma((3, C)),
                dma((3, g)),
                dma((3, g, half)),
                dma((3, g, half)),
            ],
            compiler_params=pltpu.CompilerParams(collective_id=0, has_side_effects=True),
        )(inverse_pool, panel_one, panel_two, upper_two, lower_one, lower_two, list_one, list_two)

    return jax.shard_map(
        local,
        mesh=mesh,
        in_specs=(
            P("prow", "pcol"),
            P(("prow", "pcol"), None),
            P(("prow", "pcol"), None),
            P(),
            P(),
            P(),
            P(),
            P(),
        ),
        out_specs=(P(("prow", "pcol"), None), P(), P(("prow", "pcol"), None), P(), P()),
        check_vma=False,
    )
```

time: 108 us -> 91.5 us (0.85)
  the two profiles are of different devices: /device:TPU:7 before, /device:TPU:0 now
where the time goes in v2:
time: 91.5 us; the launch traced here: 91.3 us
  Pallas kernels  83.5 us (91%)
  local copies, waits for them, and re-layouts  7.12 us (8%)
    pallas_call x1, Pallas kernels, local(): pl.pallas_call(functools.partial(body, R, C, nsend), out_shape=(strip, bl...  83.5 us
    unnamed x11, local copies, waits for them, and re-layouts  7.12 us

profile of v2, /device:TPU:0, one launch (start us, length us, event | category | flops | bytes accessed | tf_op | source)
XLA Modules:
  0.0 91.3 jit_solution(12871920239474194933)
XLA Ops:
  0.6 83.5 %shard_map.119 = (f32[48,512]{1,0:T(8,128)}, f32[512,512]{1,0:T(8,128)}, f32[48,512]{1,0:T(8,128)}, f32[512,512]{1,0:T(8,128)}, f32[512,512]{1,0:T(8,128)}) custom-call(f32[192,384]{1,0:T(8,128)} %x_in.1, f32[48,512]{1,0:T(8,128)} %one_in.1, f32[48,512]{1,0:T(8,128)} %two_in.1, f32[512,512]{1,0:T(8,128)} %u_in.1, f32[512,512]{1,0:T(8,128)} %l1_in.1, ...), custom_call_target="tpu_custom_call" | custom-call | tf_op jit(solution)/shard_map/pallas_call | solution.py:353
  84.2 1.5 %copy.18 = f32[48,512]{1,0:T(8,128)} copy(f32[48,512]{1,0:T(8,128)} %get-tuple-element.10) | data formatting | bytes 196608
  85.7 0.0 copy-start.2
  85.7 0.0 copy-start.1
  85.7 2.4 %copy.19 = f32[512,512]{1,0:T(8,128)} copy(f32[512,512]{1,0:T(8,128)} %get-tuple-element.11) | data formatting | bytes 2097152
  88.1 0.0 copy-done.2
  88.1 0.6 copy.20
  88.7 0.0 copy-done.1
  88.7 0.0 copy-start
  88.7 1.0 %copy.21 = f32[512,512]{1,0:T(8,128)} copy(f32[512,512]{1,0:T(8,128)S(1)} %copy-done.1) | data formatting | bytes 2097152
  89.7 0.6 copy-done
  90.3 1.0 %copy.22 = f32[512,512]{1,0:T(8,128)} copy(f32[512,512]{1,0:T(8,128)S(1)} %copy-done) | data formatting | bytes 2097152
Async XLA Ops:
  85.7 2.4 %copy-start.2 = (f32[48,512]{1,0:T(8,128)S(1)}, f32[48,512]{1,0:T(8,128)}, u32[]{:S(2)}) copy-start(f32[48,512]{1,0:T(8,128)} %get-tuple-element.12) | copy-start | bytes 294916
  85.7 3.0 %copy-start.1 = (f32[512,512]{1,0:T(8,128)S(1)}, f32[512,512]{1,0:T(8,128)}, u32[]{:S(2)}) copy-start(f32[512,512]{1,0:T(8,128)} %get-tuple-element.13) | copy-start | bytes 3145732
  88.7 1.6 %copy-start = (f32[512,512]{1,0:T(8,128)S(1)}, f32[512,512]{1,0:T(8,128)}, u32[]{:S(2)}) copy-start(f32[512,512]{1,0:T(8,128)} %get-tuple-element.14) | copy-start | bytes 3145732

commit v3 on v2

--- a/solution.py
+++ b/solution.py
@@ -35,6 +35,15 @@
         return jnp.maximum(hits, jnp.where(blocks == listing[k], 1.0, 0.0).astype(jnp.float32))
 
     return lax.fori_loop(0, listing.shape[0], step, jnp.zeros((count, 1), jnp.float32))
+
+
+def write_out(*refs):
+    sems = refs[-1]
+    copies = [pltpu.make_async_copy(refs[k], refs[5 + k], sems.at[k]) for k in range(5)]
+    for copy in copies:
+        copy.start()
+    for copy in copies:
+        copy.wait()
 
 
 def body(
@@ -97,15 +106,18 @@
             peers += 1
     pl.semaphore_wait(barrier, peers)
 
-    def to_columns(k, dz):
-        plane = (z + C - dz) % C
-        src = panels[k] if dz == 0 else zbuf.at[k, dz]
+    def to_columns(k, src, plane, valid=True):
         own = i * C + c
         dst, sem = at(mcol.at[k], own, span), m_sem.at[k, own]
-        send(src, dst, sem, (p, plane), plane != c)
-        pl.when(plane == c)(pltpu.make_async_copy(src, dst, sem).start)
+        send(src, dst, sem, (p, plane), (plane != c) & valid)
+        pl.when((plane == c) & valid)(pltpu.make_async_copy(src, dst, sem).start)
         for di in range(1, g):
-            send(src, dst, sem, (z * g + (i + di) % g, plane), plane // 2 == c // 2)
+            to = (z * g + (i + di) % g, plane)
+            send(src, dst, sem, to, (plane // 2 == c // 2) & valid)
+
+    def along(k, src, plane, way, valid=True):
+        inside = (z + 1 < C) if way > 0 else (z > 0)
+        send(src, zbuf.at[k, plane], z_sem.at[k, plane], plane_peer(way % C), inside & valid)
 
     def far(dy, parity):
         return ((c // 2 + dy) % half) * 2 + parity
@@ -209,31 +221,59 @@
         for dz in range(1, C):
             send(piece, piece, gz_sem.at[b, dz], plane_peer(dz))
 
-    def onward(b, di):
-        piece = block_part(b, c, (i + g - di) % g)
+    def gram_part(b, di, dc, base):
+        return block_part(b, (base + C - dc) % C, (i + g - di) % g)
+
+    def to_side(b, dc):
+        piece = gram_part(b, 0, dc, c)
+        for di in range(1, g):
+            send(piece, piece, gx_sem.at[b, di, dc // 2], side_peer(di))
+
+    def to_rows(b, di):
+        piece = gram_part(b, di, 0, c)
         for dc in range(2, C, 2):
             send(piece, piece, gy_sem.at[b, di, dc // 2], (p, (c + dc) % C))
-        send(piece, piece, gc_sem.at[b, di, 0], (p, partner))
+
+    def to_partner(b, di, dc):
+        piece = gram_part(b, di, dc, c)
+        send(piece, piece, gc_sem.at[b, di, dc // 2], (p, partner))
+
+    def side_arrived(b, di, dc):
+        arrived(gram_part(b, di, dc, c), gx_sem.at[b, di, dc // 2])
+
+    def rows_arrived(b, di, dc):
+        arrived(gram_part(b, di, dc, c), gy_sem.at[b, di, dc // 2])
 
     def gather_side(b):
         for dz in range(1, C):
             arrived(block(b, c, i, (z + C - dz) % C), gz_sem.at[b, dz])
-        piece = block_part(b, c, i)
-        for di in range(1, g):
-            send(piece, piece, gx_sem.at[b, di], side_peer(di))
-        onward(b, 0)
+        to_side(b, 0)
+        to_rows(b, 0)
+        to_partner(b, 0, 0)
 
     def gather_row(b):
-        for di in range(1, g):
-            arrived(block_part(b, c, (i + g - di) % g), gx_sem.at[b, di])
-            onward(b, di)
+        if b == 1:
+            for dc in range(2, C, 2):
+                rows_arrived(b, 0, dc)
+                to_side(b, dc)
+                to_partner(b, 0, dc)
+        else:
+            for di in range(1, g):
+                side_arrived(b, di, 0)
+                to_rows(b, di)
+                to_partner(b, di, 0)
 
     def gather_core(b):
-        for di in range(g):
-            for dc in range(2, C, 2):
-                piece = block_part(b, (c + C - dc) % C, (i + g - di) % g)
-                arrived(piece, gy_sem.at[b, di, dc // 2])
-                send(piece, piece, gc_sem.at[b, di, dc // 2], (p, partner))
+        if b == 1:
+            for di in range(1, g):
+                for dc in range(0, C, 2):
+                    side_arrived(b, di, dc)
+                    to_partner(b, di, dc)
+        else:
+            for di in range(g):
+                for dc in range(2, C, 2):
+                    rows_arrived(b, di, dc)
+                    to_partner(b, di, dc)
 
     def gathered(b):
         for di in range(g):
@@ -242,9 +282,9 @@
                 arrived(piece, gc_sem.at[b, di, dc // 2])
 
     for k in range(2):
-        for dz in range(1, C):
-            send(panels[k], zbuf.at[k, dz], z_sem.at[k, dz], plane_peer(dz))
-        to_columns(k, 0)
+        along(k, panels[k], z, 1)
+        along(k, panels[k], z, -1)
+        to_columns(k, panels[k], z)
     for copy in loads[:2]:
         copy.wait()
     for src, dst in ((l1_v, d1_out), (l2_v, d2_out)):
@@ -252,8 +292,14 @@
         dst[...] = split_dot(pair, pair, FIRST)
     for k in range(2):
         for dz in range(1, C):
-            arrived(zbuf.at[k, dz], z_sem.at[k, dz])
-            to_columns(k, dz)
+            for way in (1, -1):
+                valid = (z >= dz) if way > 0 else (z + dz < C)
+                plane = (z + C - way * dz) % C
+                src, sem = zbuf.at[k, plane], z_sem.at[k, plane]
+                pl.when(valid)(functools.partial(arrived, src, sem))
+                if dz < C - 1:
+                    along(k, src, plane, way, valid)
+                to_columns(k, src, plane, valid)
         to_row(k)
         if k == 0:
             across(0)
@@ -327,7 +373,7 @@
     for cc in range(C):
         d2_out[:, cc * wc:(cc + 1) * wc] += qfull[cc, 2 * W:3 * W]
 
-    assert len(pending) == nsend, len(pending)
+    assert len(pending) <= nsend
     for copy, when in pending:
         if when is None:
             copy.wait_send()
@@ -343,16 +389,15 @@
         span, W = panel_one.shape
         rows, K = inverse_pool.shape
         wc, half = W // C, C // 2
-        panel = (C - 1) + C * g + 2 * (half - 1) * (g - 1) + half + (half - 1)
+        panel = 2 * (C - 1) + (2 * C - 1) * g + 2 * (half - 1) * (g - 1) + half + (half - 1)
         reduced = half + (half - 1) + (C - 1)
         gram = (g - 1) + 2 * (C - 1) + (g - 1) + g * half + g * (half - 1)
         nsend = 2 * panel + 2 * reduced + 3 * gram
         f32, dma = jnp.float32, pltpu.SemaphoreType.DMA
-        block = jax.ShapeDtypeStruct((W, W), f32)
-        strip = jax.ShapeDtypeStruct((span, W), f32)
-        return pl.pallas_call(
+        shapes = ((span, W), (W, W), (span, W), (W, W), (W, W))
+        results = pl.pallas_call(
             functools.partial(body, R, C, nsend),
-            out_shape=(strip, block, strip, block, block),
+            out_shape=tuple(pltpu.VMEM(shape, f32) for shape in shapes),
             in_specs=[pl.BlockSpec(memory_space=pl.ANY)] * 6
             + [pl.BlockSpec(memory_space=pltpu.SMEM)] * 2,
             out_specs=(pl.BlockSpec(memory_space=pltpu.VMEM),) * 5,
@@ -386,12 +431,20 @@
                 dma((3, g)),
                 dma((3, C)),
                 dma((3, C)),
-                dma((3, g)),
+                dma((3, g, half)),
                 dma((3, g, half)),
                 dma((3, g, half)),
             ],
             compiler_params=pltpu.CompilerParams(collective_id=0, has_side_effects=True),
         )(inverse_pool, panel_one, panel_two, upper_two, lower_one, lower_two, list_one, list_two)
+        return pl.pallas_call(
+            write_out,
+            out_shape=tuple(jax.ShapeDtypeStruct(shape, f32) for shape in shapes),
+            in_specs=[pl.BlockSpec(memory_space=pl.ANY)] * 5,
+            out_specs=(pl.BlockSpec(memory_space=pl.ANY),) * 5,
+            scratch_shapes=[dma((5,))],
+            compiler_params=pltpu.CompilerParams(vmem_limit_bytes=8 * W * W * 4),
+        )(*results)
 
     return jax.shard_map(
         local,

time: 91.5 us -> 79.8 us (0.87)
  local copies, waits for them, and re-layouts: 7.12 us -> 0 us
  Pallas kernels: 83.5 us -> 79 us
    unnamed x11 -> x0, local copies, waits for them, and re-layouts: 7.12 us -> none
    pallas_call x1 -> x2, Pallas kernels: 83.5 us -> 79 us  [the longest x1 77.2 us: local(): pl.pallas_call(functools.partial(body, R, C, nsend), out_shape=tuple((plt...]
where the time goes in v3:
time: 79.8 us; the launch traced here: 79.6 us
  Pallas kernels  79 us (99%)
    pallas_call x1, Pallas kernels, local(): pl.pallas_call(functools.partial(body, R, C, nsend), out_shape=tuple((plt...  77.2 us
    pallas_call x1, Pallas kernels, local(): pl.pallas_call(write_out, out_shape=tuple((jax.ShapeDtypeStruct(shape, f3...  1.77 us

profile of v3, /device:TPU:0, one launch (start us, length us, event | category | flops | bytes accessed | tf_op | source)
XLA Modules:
  0.0 79.6 jit_solution(1356425302369294397)
XLA Ops:
  0.6 77.2 %shard_map.119 = (f32[48,512]{1,0:T(8,128)S(1)}, f32[512,512]{1,0:T(8,128)S(1)}, f32[48,512]{1,0:T(8,128)S(1)}, f32[512,512]{1,0:T(8,128)S(1)}, f32[512,512]{1,0:T(8,128)S(1)}) custom-call(f32[192,384]{1,0:T(8,128)} %x_in.1, f32[48,512]{1,0:T(8,128)} %one_in.1, f32[48,512]{1,0:T(8,128)} %two_in.1, f32[512,512]{1,0:T(8,128)} %u_in.1, f32[512,512]{1,0:T(8,128)} %l1_in.1, ...), custom_call_target="tpu_custom_call" | custom-call | tf_op jit(solution)/shard_map/pallas_call | solution.py:398
  77.8 1.8 %shard_map.120 = (f32[48,512]{1,0:T(8,128)}, f32[512,512]{1,0:T(8,128)}, f32[48,512]{1,0:T(8,128)}, f32[512,512]{1,0:T(8,128)}, f32[512,512]{1,0:T(8,128)}) custom-call(f32[48,512]{1,0:T(8,128)S(1)} %get-tuple-element.10.refs_0_, f32[512,512]{1,0:T(8,128)S(1)} %get-tuple-element.11.refs_1_, f32[48,512]{1,0:T(8,128)S(1)} %get-tuple-element.12.refs_2_, ...), custom_call_target="tpu_custom_call" | custom-call | tf_op jit(solution)/shard_map/pallas_call | solution.py:440

commit v4 on v3

--- a/solution.py
+++ b/solution.py
@@ -285,11 +285,6 @@
         along(k, panels[k], z, 1)
         along(k, panels[k], z, -1)
         to_columns(k, panels[k], z)
-    for copy in loads[:2]:
-        copy.wait()
-    for src, dst in ((l1_v, d1_out), (l2_v, d2_out)):
-        pair = halves(src[...])
-        dst[...] = split_dot(pair, pair, FIRST)
     for k in range(2):
         for dz in range(1, C):
             for way in (1, -1):
@@ -317,6 +312,11 @@
     right_one = total(0, row_one)
     qbuf[0] = split_dot(left, right_one, FIRST)
     side_out(0)
+    for copy in loads[:2]:
+        copy.wait()
+    for src, dst in ((l1_v, d1_out), (l2_v, d2_out)):
+        pair = halves(src[...])
+        dst[...] = split_dot(pair, pair, FIRST)
     tile_product(1, list2)
     pair_sum(1)
     row_arrived(1)

time: 79.8 us -> 79.8 us (level)
  no operation moved by 1% of the time
where the time goes in v4:
time: 79.8 us; the launch traced here: 79.6 us
  Pallas kernels  79 us (99%)
    pallas_call x1, Pallas kernels, local(): pl.pallas_call(functools.partial(body, R, C, nsend), out_shape=tuple((plt...  77.2 us
    pallas_call x1, Pallas kernels, local(): pl.pallas_call(write_out, out_shape=tuple((jax.ShapeDtypeStruct(shape, f3...  1.77 us

profile of v4, /device:TPU:0, one launch (start us, length us, event | category | flops | bytes accessed | tf_op | source)
XLA Modules:
  0.0 79.6 jit_solution(17197226222745749315)
XLA Ops:
  0.6 77.2 %shard_map.119 = (f32[48,512]{1,0:T(8,128)S(1)}, f32[512,512]{1,0:T(8,128)S(1)}, f32[48,512]{1,0:T(8,128)S(1)}, f32[512,512]{1,0:T(8,128)S(1)}, f32[512,512]{1,0:T(8,128)S(1)}) custom-call(f32[192,384]{1,0:T(8,128)} %x_in.1, f32[48,512]{1,0:T(8,128)} %one_in.1, f32[48,512]{1,0:T(8,128)} %two_in.1, f32[512,512]{1,0:T(8,128)} %u_in.1, f32[512,512]{1,0:T(8,128)} %l1_in.1, ...), custom_call_target="tpu_custom_call" | custom-call | tf_op jit(solution)/shard_map/pallas_call | solution.py:398
  77.8 1.8 %shard_map.120 = (f32[48,512]{1,0:T(8,128)}, f32[512,512]{1,0:T(8,128)}, f32[48,512]{1,0:T(8,128)}, f32[512,512]{1,0:T(8,128)}, f32[512,512]{1,0:T(8,128)}) custom-call(f32[48,512]{1,0:T(8,128)S(1)} %get-tuple-element.10.refs_0_, f32[512,512]{1,0:T(8,128)S(1)} %get-tuple-element.11.refs_1_, f32[48,512]{1,0:T(8,128)S(1)} %get-tuple-element.12.refs_2_, ...), custom_call_target="tpu_custom_call" | custom-call | tf_op jit(solution)/shard_map/pallas_call | solution.py:440
